TPU v7x, 256 devices: a whole 4x4x8 slice. The times are simulated.
256 devices in a mesh: aux: 2 (over core), row: 8 (over z), col: 16 (over x, y).
Axes of the slice: x: 4, y: 4, z: 8, core: 2. Of those that a mesh axis runs over, the one named last changes fastest.
Arguments:
- coulomb: bfloat16 [64, 2048, 2048], P('aux', 'row', 'col'), may hold values from -6 to 6
- occupied: bfloat16 [2048, 2048], P('row'), may hold values from -0.125 to 0.125
- virtual: bfloat16 [2048, 2048], P('row'), may hold values from -0.125 to 0.125
- tile_mask: int32 [16, 16], replicated, may hold values 0 or 1
Outputs:
- chi: float32 [64, 64], P('aux')
All inputs are finite; a program needn't handle non-finite values.
Results may differ from a plain program's by a relative error of at most 0.0042.
Values may be sent and summed in bfloat16 or wider, within the bound.
A program may use at most 128 MiB of HBM per device.

v0:
```python
import jax
import jax.numpy as jnp
from jax import lax
from jax.sharding import PartitionSpec as P

NAO = 2048
TILE = 128


def swapped(value, axis, apart):
    mask = 2**apart
    pairs = [(source, source ^ mask) for source in range(lax.axis_size(axis))]
    return lax.ppermute(value, axis, pairs)


def shards(coulomb, occupied, virtual, tile_mask):
    rows = lax.axis_size("row")
    cols = lax.axis_size("col")
    pdev, mrow, ncol = coulomb.shape
    nao = mrow * rows
    row_idx = lax.axis_index("row")
    col_idx = lax.axis_index("col")
    aux_idx = lax.axis_index("aux")
    tiles_r = mrow // TILE
    tiles_c = ncol // TILE
    local_tiles = lax.dynamic_slice(
        tile_mask, (row_idx * tiles_r, col_idx * tiles_c), (tiles_r, tiles_c)
    )
    local_mask = jnp.repeat(jnp.repeat(local_tiles, TILE, axis=0), TILE, axis=1).astype(
        jnp.bfloat16
    )
    screened = coulomb * local_mask[None]
    moved = lax.all_to_all(screened, "row", split_axis=0, concat_axis=1, tiled=True)
    pieces = moved.shape[0]
    occ_all, virt_all = (
        lax.all_gather(occupied, "row", axis=0, tiled=True),
        lax.all_gather(virtual, "row", axis=0, tiled=True),
    )
    half = jnp.einsum("ml,pmn->pln", occ_all, moved, preferred_element_type=jnp.float32).astype(
        jnp.bfloat16
    )
    jpart = mrow // cols
    shaped = half.reshape(pieces, rows, cols, jpart, ncol)
    spread = lax.all_to_all(shaped, "col", split_axis=2, concat_axis=4, tiled=True)
    spread = spread.reshape(pieces, rows * jpart, nao)
    dressed = jnp.einsum(
        "pln,ns->pls", spread, virt_all, preferred_element_type=jnp.float32
    ).astype(jnp.bfloat16)
    layered = dressed.reshape(pieces, rows, 1, jpart, cols, ncol)
    returned = lax.all_to_all(
        lax.all_to_all(layered, "row", split_axis=1, concat_axis=0, tiled=True),
        "col",
        split_axis=4,
        concat_axis=2,
        tiled=True,
    )
    aligned = returned.reshape(pdev, mrow, ncol)
    theirs = swapped(screened, "aux", 0)
    with_mine = jnp.einsum("pls,qls->pq", aligned, screened, preferred_element_type=jnp.float32)
    with_theirs = jnp.einsum("pls,qls->pq", aligned, theirs, preferred_element_type=jnp.float32)
    first_half = jnp.where(aux_idx == 0, with_mine, with_theirs)
    second_half = jnp.where(aux_idx == 0, with_theirs, with_mine)
    partial_chi = jnp.concatenate([first_half, second_half], axis=1)
    slots = lax.axis_size("aux")
    placed = jnp.zeros((slots,) + partial_chi.shape, partial_chi.dtype)
    placed = lax.dynamic_update_index_in_dim(placed, partial_chi, aux_idx, 0)
    total = lax.psum(placed, ("aux", "row", "col"))
    total_chi = lax.dynamic_index_in_dim(total, aux_idx, 0, keepdims=False)
    return total_chi / NAO


def solution(mesh):
    placed = (P("aux", "row", "col"), P("row", None), P("row", None), P())
    return jax.shard_map(
        shards, mesh=mesh, in_specs=placed, out_specs=P("aux", None), check_vma=False
    )
```

profile of v0, /device:TPU:1, one launch (start us, length us, event | category | flops | bytes accessed | tf_op | source)
XLA Modules:
  0.0 430.4 jit_solution(17136864265026919637)
XLA Ops:
  6.5 0.0 all-gather.3.cloned.1.call-start
  6.5 0.7 all-gather.3.cloned.1.call-update
  7.3 0.0 all-gather.5.cloned.1.call-start
  7.3 0.7 all-gather.5.cloned.1.call-update
  8.0 0.9 fusion.14
  8.9 0.1 broadcast_bitcast_fusion
  9.0 2.8 copy_multiply_fusion
  11.7 0.8 copy.15
  12.6 79.7 %all_to_all.66 = bf16[32,256,128]{2,1,0:T(8,128)(2,1)} all-to-all(bf16[32,256,128]{2,1,0:T(8,128)(2,1)S(1)} %copy.15), channel_id=1, replica_groups=mesh['aux'=2,'row'=8,'col'=16] {'row'}, dimensions={0} | all-to-all | bytes 4194304 | tf_op jit(solution)/shard_map/all_to_all | solution.py:33
  92.2 4.5 %copy.16 = bf16[8,4,256,128]{2,0,3,1:T(8,128)(2,1)} copy(bf16[8,4,256,128]{3,2,1,0:T(8,128)(2,1)} %bitcast.62) | data formatting | bytes 4194304 | tf_op jit(solution)/shard_map/all_to_all | solution.py:33
  96.7 4.2 all_to_all.51
  100.9 48.7 %all-gather.3.cloned.1.call-done = bf16[2048,2048]{1,0:T(8,128)(2,1)} async-done(((bf16[256,2048]{1,0:T(8,128)(2,1)}), bf16[2048,2048]{1,0:T(8,128)(2,1)}) %all-gather.3.cloned.1.call-update) | async-done | bytes 8388624 | tf_op jit(solution)/shard_map/all_gather | solution.py:36
  149.7 9.8 %fusion.10 = bf16[4,2048,128]{1,2,0:T(8,128)(2,1)} fusion(bf16[4,2048,128]{1,2,0:T(8,128)(2,1)} %all_to_all.51, bf16[2048,2048]{1,0:T(8,128)(2,1)} %all-gather.3.cloned.1.call-done), kind=kOutput, calls=%fused_computation.6 | convolution fusion | flops 4296015872 | bytes 12582912 | tf_op jit(solution)/shard_map/ml,pmn->pln/dot_general | solution.py:39
  159.5 4.0 copy.17
  163.4 2.2 copy.18
  165.6 33.7 %all_to_all.67 = bf16[4,8,16,16,128]{4,3,1,0,2:T(8,128)(2,1)S(1)} all-to-all(bf16[4,8,16,16,128]{4,3,1,0,2:T(8,128)(2,1)S(1)} %copy.18), channel_id=1, replica_groups=mesh['aux'=2,'row'=8,'col'=16] {'col'}, dimensions={2} | all-to-all | bytes 4194304 | tf_op jit(solution)/shard_map/all_to_all | solution.py:44
  199.3 3.7 copy.19
  203.1 4.2 reshape.37
  207.3 37.2 %all-gather.5.cloned.1.call-done = bf16[2048,2048]{1,0:T(8,128)(2,1)} async-done(((bf16[256,2048]{1,0:T(8,128)(2,1)}), bf16[2048,2048]{1,0:T(8,128)(2,1)}) %all-gather.5.cloned.1.call-update) | async-done | bytes 8388624 | tf_op jit(solution)/shard_map/all_gather | solution.py:37
  244.4 8.5 %fusion.7 = bf16[4,128,2048]{2,1,0:T(8,128)(2,1)S(1)} fusion(bf16[4,128,2048]{2,1,0:T(8,128)(2,1)} %reshape.37, bf16[2048,2048]{1,0:T(8,128)(2,1)} %all-gather.5.cloned.1.call-done), kind=kOutput, calls=%fused_computation.5 | convolution fusion | flops 4296015872 | bytes 12582912 | tf_op jit(solution)/shard_map/pln,ns->pls/dot_general | solution.py:46
  253.0 0.6 copy.23
  253.6 0.6 copy.20
  254.2 53.5 %all_to_all.68 = bf16[4,8,1,16,16,128]{5,4,3,0,2,1:T(8,128)(2,1)S(1)} all-to-all(bf16[4,8,1,16,16,128]{5,4,3,0,2,1:T(8,128)(2,1)S(1)} %copy.20), channel_id=1, replica_groups=mesh['aux'=2,'row'=8,'col'=16] {'row'}, dimensions={1} | all-to-all | bytes 4194304 | tf_op jit(solution)/shard_map/all_to_all | solution.py:51
  307.7 1.8 copy.21
  309.6 6.6 %all-to-all-start.3 = ((bf16[32,1,1,16,16,128]{5,3,0,2,1,4:T(8,128)(2,1)}), bf16[32,1,1,16,16,128]{5,3,0,2,1,4:T(8,128)(2,1)}, u32[]{:S(2)}, u32[]{:S(2)}) async-start(bf16[32,1,1,16,16,128]{5,3,0,2,1,4:T(8,128)(2,1)} %copy.21), calls=%async_computation.3 | async-start | bytes 4194304 | tf_op jit(solution)/shard_map/all_to_all | solution.py:50
  316.2 2.8 collective-permute-start
  319.0 22.5 %all-to-all-done.3 = bf16[32,1,1,16,16,128]{5,3,0,2,1,4:T(8,128)(2,1)} async-done(((bf16[32,1,1,16,16,128]{5,3,0,2,1,4:T(8,128)(2,1)}), bf16[32,1,1,16,16,128]{5,3,0,2,1,4:T(8,128)(2,1)}, u32[]{:S(2)}, u32[]{:S(2)}) %all-to-all-start.3) | async-done | bytes 2097184 | tf_op jit(solution)/shard_map/all_to_all | solution.py:50
  341.5 2.1 copy.22
  343.6 0.7 convolution_bitcast_fusion.1
  344.3 0.0 collective-permute-done
  344.3 2.3 broadcast_select_fusion.1
  346.6 0.1 fusion.13
  346.7 76.2 %psum.7 = f32[2,32,64]{2,1,0:T(8,128)S(1)} all-reduce(f32[2,32,64]{2,1,0:T(8,128)S(1)} %fusion.13), channel_id=1, replica_groups=mesh['aux'=2,'row'=8,'col'=16] {'aux','row','col'}, use_global_device_ids=true, to_apply=%region_0.1 | all-reduce | flops 4096 | bytes 32768 | tf_op jit(solution)/shard_map/psum | solution.py:67
  422.9 0.6 multiply_bitcast_fusion
  (1 shorter events, 0.0 us)
Async XLA Ops:
  6.5 143.1 %all-gather.3.cloned.1.call-start = ((), (), s32[]{:S(2)}) async-start(), calls=%async_computation.4 | async-start | bytes 9437184 | tf_op jit(solution)/shard_map/all_gather | solution.py:36
  7.3 237.2 %all-gather.5.cloned.1.call-start = ((), (), s32[]{:S(2)}) async-start(), calls=%async_computation.5 | async-start | bytes 9437184 | tf_op jit(solution)/shard_map/all_gather | solution.py:37
  309.6 31.9 %all-to-all-start.3 = ((bf16[32,1,1,16,16,128]{5,3,0,2,1,4:T(8,128)(2,1)}), bf16[32,1,1,16,16,128]{5,3,0,2,1,4:T(8,128)(2,1)}, u32[]{:S(2)}, u32[]{:S(2)}) async-start(bf16[32,1,1,16,16,128]{5,3,0,2,1,4:T(8,128)(2,1)} %copy.21), calls=%async_computation.3 | async-start | bytes 4194304 | tf_op jit(solution)/shard_map/all_to_all | solution.py:50
  316.2 28.2 %collective-permute-start = (bf16[32,256,128]{2,0,1:T(8,128)(2,1)S(1)}, bf16[32,256,128]{2,0,1:T(8,128)(2,1)}, u32[]{:S(2)}, u32[]{:S(2)}) collective-permute-start(bf16[32,256,128]{2,0,1:T(8,128)(2,1)S(1)} %copy_multiply_fusion), channel_id=1, source_target_pairs={{0,128},{128,0},{1,129},{129,1},{2,130},{130,2},{3,131},{131,3},{4... | collective-permute-start | bytes 6291464 | tf_op jit(solution)/shard_map/ppermute | solution.py:13
Sparse Core Ops, SparseCore 0:
  9.1 140.4 all-gather.2
  151.4 92.9 all-gather.4
where the time goes:
time: 431 us; the launch traced here: 430 us
  blocking collectives  243 us (56%)
  waiting for transfers between devices  110 us (26%)
  local copies, waits for them, and re-layouts  28.9 us (7%)
  matrix products  21.3 us (5%)
  between operations  13.5 us (3%)
  starting transfers between devices  9.44 us (2%)
  other arithmetic  4.33 us (1%)
    all_to_all x1, blocking collectives, shards(): lax.all_to_all(screened, 'row', split_axis=0, concat_axis=1, tiled=True)  79.7 us
    psum x1, blocking collectives, shards(): total = lax.psum(placed, ('aux', 'row', 'col'))  76.2 us
    all_to_all x1, blocking collectives, shards(): lax.all_to_all(layered, 'row', split_axis=1, concat_axis=0, tiled=True)  53.5 us
    all_gather x1, waiting for transfers between devices, shards(): lax.all_gather(occupied, 'row', axis=0, tiled=True)  48.7 us
    all_gather x1, waiting for transfers between devices, shards(): lax.all_gather(virtual, 'row', axis=0, tiled=True)  37.2 us
    all_to_all x1, blocking collectives, shards(): lax.all_to_all(shaped, 'col', split_axis=2, concat_axis=4, tiled=True)  33.7 us
    all_to_all x1, waiting for transfers between devices, shards(): lax.all_to_all(lax.all_to_all(layered, 'row', split_axis=1, concat_axis=0...  22.5 us
    dot_general x1, matrix products, shards(): jnp.einsum('ml,pmn->pln', occ_all, moved, preferred_element_type=jnp.floa...  9.81 us
  transfers between devices with their start and end apart: 4, of which 3 were waited for; matrix products, arithmetic and copies ran while one was open for 8% of the time, Pallas kernels for 0%

commit v1 on v0

--- a/solution.py
+++ b/solution.py
@@ -5,6 +5,24 @@
 
 NAO = 2048
 TILE = 128
+
+
+def gather_around(array, axis, dim):
+    ways, here, step = (lax.axis_size(axis), lax.axis_index(axis), array.shape[dim])
+    shape = [n * ways if d == dim else n for d, n in enumerate(array.shape)]
+    full = lax.dynamic_update_slice_in_dim(
+        jnp.zeros(shape, array.dtype), array, here * step, axis=dim
+    )
+    going_up = going_down = array
+    for far in range(1, ways // 2 + 1):
+        going_up = lax.ppermute(going_up, axis, [(d, (d + 1) % ways) for d in range(ways)])
+        full = lax.dynamic_update_slice_in_dim(full, going_up, (here - far) % ways * step, axis=dim)
+        if 2 * far < ways:
+            going_down = lax.ppermute(going_down, axis, [(d, (d - 1) % ways) for d in range(ways)])
+            full = lax.dynamic_update_slice_in_dim(
+                full, going_down, (here + far) % ways * step, axis=dim
+            )
+    return full
 
 
 def swapped(value, axis, apart):
@@ -33,7 +51,7 @@
     moved = lax.all_to_all(screened, "row", split_axis=0, concat_axis=1, tiled=True)
     pieces = moved.shape[0]
     occ_all, virt_all = (
-        lax.all_gather(occupied, "row", axis=0, tiled=True),
+        gather_around(occupied, "row", 0),
         lax.all_gather(virtual, "row", axis=0, tiled=True),
     )
     half = jnp.einsum("ml,pmn->pln", occ_all, moved, preferred_element_type=jnp.float32).astype(

time: 431 us -> 467 us (1.084)
  blocking collectives: 243 us -> 162 us
  waiting for transfers between devices: 110 us -> 191 us
  local copies, waits for them, and re-layouts: 28.9 us -> 49.4 us
  starting transfers between devices: 9.44 us -> 25.5 us
    ppermute x0 -> x7, waiting for transfers between devices: none -> 172 us  [the longest x3 119 us: gather_around(): lax.ppermute(going_down, axis, [(d, (d - 1) % ways) for d in range(ways)])]
    all_to_all x1 -> x0, blocking collectives: 79.7 us -> none  [shards(): lax.all_to_all(screened, 'row', split_axis=0, concat_axis=1, tiled=True)]
    all_gather x1 -> x0, waiting for transfers between devices: 48.7 us -> none  [shards(): lax.all_gather(occupied, 'row', axis=0, tiled=True)]
    all_gather x1, waiting for transfers between devices: 37.2 us -> 0.01 us  [shards(): lax.all_gather(virtual, 'row', axis=0, tiled=True)]
    dynamic_update_slice x0 -> x8, local copies, waits for them, and re-layouts: none -> 14.9 us  [the longest x4 8.06 us: gather_around(): lax.dynamic_update_slice_in_dim(full, going_up, (here - far) % ways * ste...]
    ppermute x0 -> x7, starting transfers between devices: none -> 8.17 us  [the longest x4 4.22 us: gather_around(): lax.ppermute(going_up, axis, [(d, (d + 1) % ways) for d in range(ways)])]
    all_to_all x0 -> x1, starting transfers between devices: none -> 7.42 us  [shards(): lax.all_to_all(screened, 'row', split_axis=0, concat_axis=1, tiled=True)]
    all_to_all x1, waiting for transfers between devices: 22.5 us -> 17.8 us  [shards(): lax.all_to_all(lax.all_to_all(layered, 'row', split_axis=1, concat_axis=0...]
  transfers between devices with their start and end apart: 4 -> 11, of which waited for: 3 -> 8; matrix products, arithmetic and copies ran while one was open for 8% -> 12% of each run, Pallas kernels for 0% -> 0%
where the time goes in v1:
time: 467 us; the launch traced here: 466 us
  waiting for transfers between devices  191 us (41%)
  blocking collectives  162 us (35%)
  local copies, waits for them, and re-layouts  49.4 us (11%)
  starting transfers between devices  25.5 us (5%)
  matrix products  20.6 us (4%)
  between operations  13.5 us (3%)
    ppermute x3, waiting for transfers between devices, gather_around(): lax.ppermute(going_down, axis, [(d, (d - 1) % ways) for d in range(ways)])  119 us
    psum x1, blocking collectives, shards(): total = lax.psum(placed, ('aux', 'row', 'col'))  78.9 us
    ppermute x4, waiting for transfers between devices, gather_around(): lax.ppermute(going_up, axis, [(d, (d + 1) % ways) for d in range(ways)])  53.6 us
    all_to_all x1, blocking collectives, shards(): lax.all_to_all(layered, 'row', split_axis=1, concat_axis=0, tiled=True)  52 us
    all_to_all x1, blocking collectives, shards(): lax.all_to_all(shaped, 'col', split_axis=2, concat_axis=4, tiled=True)  31.4 us
    all_to_all x1, waiting for transfers between devices, shards(): lax.all_to_all(lax.all_to_all(layered, 'row', split_axis=1, concat_axis=0...  17.8 us
  transfers between devices with their start and end apart: 11, of which 8 were waited for; matrix products, arithmetic and copies ran while one was open for 12% of the time, Pallas kernels for 0%

profile of v1, /device:TPU:1, one launch (start us, length us, event | category | flops | bytes accessed | tf_op | source)
XLA Modules:
  0.0 466.3 jit_solution(642719558786153577)
XLA Ops:
  6.5 0.7 all-gather.2.cloned.1.call-update
  7.3 2.5 collective-permute-start
  9.8 0.9 fusion.14
  10.7 0.1 broadcast_bitcast_fusion
  10.7 2.8 copy_multiply_fusion
  13.5 2.1 copy.15
  15.7 7.4 %all-to-all-start = ((bf16[32,256,128]{2,1,0:T(8,128)(2,1)}), bf16[32,256,128]{2,1,0:T(8,128)(2,1)}, u32[]{:S(2)}, u32[]{:S(2)}) async-start(bf16[32,256,128]{2,1,0:T(8,128)(2,1)} %copy.15), calls=%async_computation | async-start | bytes 4194304 | tf_op jit(solution)/shard_map/all_to_all | solution.py:51
  23.1 2.7 collective-permute-start.1
  25.7 19.8 %collective-permute-done = bf16[256,2048]{1,0:T(8,128)(2,1)} collective-permute-done((bf16[256,2048]{1,0:T(8,128)(2,1)}, bf16[256,2048]{1,0:T(8,128)(2,1)}, u32[]{:S(2)}, u32[]{:S(2)}) %collective-permute-start) | collective-permute-done | bytes 1048608 | tf_op jit(solution)/shard_map/ppermute | solution.py:18
  45.5 91.6 %collective-permute-done.1 = bf16[256,2048]{1,0:T(8,128)(2,1)} collective-permute-done((bf16[256,2048]{1,0:T(8,128)(2,1)S(1)}, bf16[256,2048]{1,0:T(8,128)(2,1)}, u32[]{:S(2)}, u32[]{:S(2)}) %collective-permute-start.1) | collective-permute-done | bytes 1048608 | tf_op jit(solution)/shard_map/ppermute | solution.py:21
  137.1 15.2 %collective-permute-done.2 = bf16[256,2048]{1,0:T(8,128)(2,1)} collective-permute-done((bf16[256,2048]{1,0:T(8,128)(2,1)}, bf16[256,2048]{1,0:T(8,128)(2,1)}, u32[]{:S(2)}, u32[]{:S(2)}) %collective-permute-start.2) | collective-permute-done | bytes 1048608 | tf_op jit(solution)/shard_map/ppermute | solution.py:18
  152.3 1.7 collective-permute-start.4
  153.9 4.3 broadcast_in_dim.17
  158.2 1.1 constant_dynamic-update-slice_fusion.7
  159.4 24.7 %collective-permute-done.3 = bf16[256,2048]{1,0:T(8,128)(2,1)} collective-permute-done((bf16[256,2048]{1,0:T(8,128)(2,1)}, bf16[256,2048]{1,0:T(8,128)(2,1)}, u32[]{:S(2)}, u32[]{:S(2)}) %collective-permute-start.3) | collective-permute-done | bytes 1048608 | tf_op jit(solution)/shard_map/ppermute | solution.py:21
  184.1 1.3 collective-permute-start.5
  185.3 2.3 constant_dynamic-update-slice_fusion.6
  187.7 16.5 %collective-permute-done.4 = bf16[256,2048]{1,0:T(8,128)(2,1)} collective-permute-done((bf16[256,2048]{1,0:T(8,128)(2,1)}, bf16[256,2048]{1,0:T(8,128)(2,1)}, u32[]{:S(2)}, u32[]{:S(2)}) %collective-permute-start.4) | collective-permute-done | bytes 1048608 | tf_op jit(solution)/shard_map/ppermute | solution.py:18
  204.2 2.3 constant_dynamic-update-slice_fusion.5
  206.4 2.3 constant_dynamic-update-slice_fusion.4
  208.8 2.3 constant_dynamic-update-slice_fusion.3
  211.1 2.3 constant_dynamic-update-slice_fusion.2
  213.4 2.3 collective-permute-done.5
  215.7 1.1 constant_dynamic-update-slice_fusion.1
  216.8 4.5 copy.16
  221.3 4.2 all_to_all.51
  225.5 2.1 collective-permute-done.6
  227.7 1.1 constant_dynamic-update-slice_fusion
  228.8 9.1 %fusion.10 = bf16[4,2048,128]{1,2,0:T(8,128)(2,1)} fusion(bf16[4,2048,128]{1,2,0:T(8,128)(2,1)S(1)} %copy-done, bf16[2048,2048]{1,0:T(8,128)(2,1)} %constant_dynamic-update-slice_fusion), kind=kOutput, calls=%fused_computation.6 | convolution fusion | flops 4296015872 | bytes 12582912 | tf_op jit(solution)/shard_map/ml,pmn->pln/dot_general | solution.py:57
  237.9 3.9 copy.17
  241.9 2.2 copy.18
  244.1 31.4 %all_to_all.66 = bf16[4,8,16,16,128]{4,3,1,0,2:T(8,128)(2,1)S(1)} all-to-all(bf16[4,8,16,16,128]{4,3,1,0,2:T(8,128)(2,1)S(1)} %copy.18), channel_id=1, replica_groups=mesh['aux'=2,'row'=8,'col'=16] {'col'}, dimensions={2} | all-to-all | bytes 4194304 | tf_op jit(solution)/shard_map/all_to_all | solution.py:62
  275.5 3.8 copy.19
  279.2 4.2 reshape.37
  283.4 8.5 %fusion.7 = bf16[4,128,2048]{2,1,0:T(8,128)(2,1)S(1)} fusion(bf16[4,128,2048]{2,1,0:T(8,128)(2,1)} %reshape.37, bf16[2048,2048]{1,0:T(8,128)(2,1)} %all-gather.2.cloned.1.call-done), kind=kOutput, calls=%fused_computation.5 | convolution fusion | flops 4296015872 | bytes 12582912 | tf_op jit(solution)/shard_map/pln,ns->pls/dot_general | solution.py:64
  291.9 0.6 copy.23
  292.5 0.6 copy.20
  293.1 52.0 %all_to_all.67 = bf16[4,8,1,16,16,128]{5,4,3,0,2,1:T(8,128)(2,1)S(1)} all-to-all(bf16[4,8,1,16,16,128]{5,4,3,0,2,1:T(8,128)(2,1)S(1)} %copy.20), channel_id=1, replica_groups=mesh['aux'=2,'row'=8,'col'=16] {'row'}, dimensions={1} | all-to-all | bytes 4194304 | tf_op jit(solution)/shard_map/all_to_all | solution.py:69
  345.2 1.9 copy.21
  347.0 4.4 all-to-all-start.3
  351.5 5.5 %collective-permute-start.7 = (bf16[32,256,128]{2,0,1:T(8,128)(2,1)S(1)}, bf16[32,256,128]{2,0,1:T(8,128)(2,1)}, u32[]{:S(2)}, u32[]{:S(2)}) collective-permute-start(bf16[32,256,128]{2,0,1:T(8,128)(2,1)S(1)} %copy_multiply_fusion), channel_id=1, source_target_pairs={{0,128},{128,0},{1,129},{129,1},{2,130},{130,2},{3,131},{131,3},{4... | collective-permute-start | bytes 6291464 | tf_op jit(solution)/shard_map/ppermute | solution.py:31
  357.0 17.8 %all-to-all-done.3 = bf16[32,1,1,16,16,128]{5,3,0,2,1,4:T(8,128)(2,1)} async-done(((bf16[32,1,1,16,16,128]{5,3,0,2,1,4:T(8,128)(2,1)}), bf16[32,1,1,16,16,128]{5,3,0,2,1,4:T(8,128)(2,1)}, u32[]{:S(2)}, u32[]{:S(2)}) %all-to-all-start.3) | async-done | bytes 2097184 | tf_op jit(solution)/shard_map/all_to_all | solution.py:68
  374.7 2.1 copy.22
  376.9 0.7 convolution_bitcast_fusion.1
  377.6 2.3 broadcast_select_fusion.1
  379.9 0.1 fusion.13
  380.0 78.9 %psum.7 = f32[2,32,64]{2,1,0:T(8,128)S(1)} all-reduce(f32[2,32,64]{2,1,0:T(8,128)S(1)} %fusion.13), channel_id=1, replica_groups=mesh['aux'=2,'row'=8,'col'=16] {'aux','row','col'}, use_global_device_ids=true, to_apply=%region_0.1 | all-reduce | flops 4096 | bytes 32768 | tf_op jit(solution)/shard_map/psum | solution.py:85
  458.8 0.6 multiply_bitcast_fusion
  (12 shorter events, 0.0 us)
Async XLA Ops:
  6.5 276.9 %all-gather.2.cloned.1.call-start = ((), (), s32[]{:S(2)}) async-start(), calls=%async_computation.4 | async-start | bytes 9437184 | tf_op jit(solution)/shard_map/all_gather | solution.py:55
  7.3 38.3 %collective-permute-start = (bf16[256,2048]{1,0:T(8,128)(2,1)}, bf16[256,2048]{1,0:T(8,128)(2,1)}, u32[]{:S(2)}, u32[]{:S(2)}) collective-permute-start(bf16[256,2048]{1,0:T(8,128)(2,1)} %param.5), channel_id=1, source_target_pairs={{0,16},{16,32},{32,48},{48,64},{64,80},{80,96},{96,112},{112,0},{1... | collective-permute-start | bytes 3145736 | tf_op jit(solution)/shard_map/ppermute | solution.py:18
  15.6 7.4 %copy-start.1 = (bf16[256,2048]{1,0:T(8,128)(2,1)S(1)}, bf16[256,2048]{1,0:T(8,128)(2,1)}, u32[]{:S(2)}) copy-start(bf16[256,2048]{1,0:T(8,128)(2,1)} %param.5) | copy-start | bytes 3145732
  15.7 201.2 %all-to-all-start = ((bf16[32,256,128]{2,1,0:T(8,128)(2,1)}), bf16[32,256,128]{2,1,0:T(8,128)(2,1)}, u32[]{:S(2)}, u32[]{:S(2)}) async-start(bf16[32,256,128]{2,1,0:T(8,128)(2,1)} %copy.15), calls=%async_computation | async-start | bytes 4194304 | tf_op jit(solution)/shard_map/all_to_all | solution.py:51
  23.1 114.0 %collective-permute-start.1 = (bf16[256,2048]{1,0:T(8,128)(2,1)S(1)}, bf16[256,2048]{1,0:T(8,128)(2,1)}, u32[]{:S(2)}, u32[]{:S(2)}) collective-permute-start(bf16[256,2048]{1,0:T(8,128)(2,1)S(1)} %copy-done.1), channel_id=1, source_target_pairs={{0,112},{16,0},{32,16},{48,32},{64,48},{80,64},{96,80},{112,96},{1... | collective-permute-start | bytes 3145736 | tf_op jit(solution)/shard_map/ppermute | solution.py:21
  45.5 106.7 %collective-permute-start.2 = (bf16[256,2048]{1,0:T(8,128)(2,1)}, bf16[256,2048]{1,0:T(8,128)(2,1)}, u32[]{:S(2)}, u32[]{:S(2)}) collective-permute-start(bf16[256,2048]{1,0:T(8,128)(2,1)} %collective-permute-done), channel_id=1, source_target_pairs={{0,16},{16,32},{32,48},{48,64},{64,80},{80,96},{96,112},{112,0},{1... | collective-permute-start | bytes 3145736 | tf_op jit(solution)/shard_map/ppermute | solution.py:18
  137.1 47.0 %collective-permute-start.3 = (bf16[256,2048]{1,0:T(8,128)(2,1)}, bf16[256,2048]{1,0:T(8,128)(2,1)}, u32[]{:S(2)}, u32[]{:S(2)}) collective-permute-start(bf16[256,2048]{1,0:T(8,128)(2,1)} %collective-permute-done.1), channel_id=1, source_target_pairs={{0,112},{16,0},{32,16},{48,32},{64,48},{80,64},{96,80},{112,96},{1... | collective-permute-start | bytes 3145736 | tf_op jit(solution)/shard_map/ppermute | solution.py:21
  152.3 51.9 %collective-permute-start.4 = (bf16[256,2048]{1,0:T(8,128)(2,1)}, bf16[256,2048]{1,0:T(8,128)(2,1)}, u32[]{:S(2)}, u32[]{:S(2)}) collective-permute-start(bf16[256,2048]{1,0:T(8,128)(2,1)} %collective-permute-done.2), channel_id=1, source_target_pairs={{0,16},{16,32},{32,48},{48,64},{64,80},{80,96},{96,112},{112,0},{1... | collective-permute-start | bytes 3145736 | tf_op jit(solution)/shard_map/ppermute | solution.py:18
  184.1 31.7 %collective-permute-start.5 = (bf16[256,2048]{1,0:T(8,128)(2,1)}, bf16[256,2048]{1,0:T(8,128)(2,1)S(1)}, u32[]{:S(2)}, u32[]{:S(2)}) collective-permute-start(bf16[256,2048]{1,0:T(8,128)(2,1)} %collective-permute-done.3), channel_id=1, source_target_pairs={{0,112},{16,0},{32,16},{48,32},{64,48},{80,64},{96,80},{112,96},{1... | collective-permute-start | bytes 3145736 | tf_op jit(solution)/shard_map/ppermute | solution.py:21
  204.1 23.5 %collective-permute-start.6 = (bf16[256,2048]{1,0:T(8,128)(2,1)}, bf16[256,2048]{1,0:T(8,128)(2,1)S(1)}, u32[]{:S(2)}, u32[]{:S(2)}) collective-permute-start(bf16[256,2048]{1,0:T(8,128)(2,1)} %collective-permute-done.4), channel_id=1, source_target_pairs={{0,16},{16,32},{32,48},{48,64},{64,80},{80,96},{96,112},{112,0},{1... | collective-permute-start | bytes 3145736 | tf_op jit(solution)/shard_map/ppermute | solution.py:18
  225.5 3.3 copy-start
  347.0 27.7 %all-to-all-start.3 = ((bf16[32,1,1,16,16,128]{5,3,0,2,1,4:T(8,128)(2,1)}), bf16[32,1,1,16,16,128]{5,3,0,2,1,4:T(8,128)(2,1)}, u32[]{:S(2)}, u32[]{:S(2)}) async-start(bf16[32,1,1,16,16,128]{5,3,0,2,1,4:T(8,128)(2,1)} %copy.21), calls=%async_computation.3 | async-start | bytes 4194304 | tf_op jit(solution)/shard_map/all_to_all | solution.py:68
  351.5 26.1 %collective-permute-start.7 = (bf16[32,256,128]{2,0,1:T(8,128)(2,1)S(1)}, bf16[32,256,128]{2,0,1:T(8,128)(2,1)}, u32[]{:S(2)}, u32[]{:S(2)}) collective-permute-start(bf16[32,256,128]{2,0,1:T(8,128)(2,1)S(1)} %copy_multiply_fusion), channel_id=1, source_target_pairs={{0,128},{128,0},{1,129},{129,1},{2,130},{130,2},{3,131},{131,3},{4... | collective-permute-start | bytes 6291464 | tf_op jit(solution)/shard_map/ppermute | solution.py:31
Sparse Core Ops, SparseCore 0:
  9.1 196.5 all-gather.1
